TPU v7x, 256 devices: a whole 4x4x8 slice. The times are simulated.
256 devices in a mesh: src: 2 (over y_lo), tx: 8 (over y_hi, x), ty: 16 (over z, core).
Axes of the slice: x: 4, y: 4 (y_hi: 2, y_lo: 2; y = y_hi * 2 + y_lo), z: 8, core: 2. Of those that a mesh axis runs over, the one named last changes fastest.
Arguments:
- orders: float32 [8, 2, 512, 512], P('src', None, 'tx', 'ty'), may hold values from -0.00390625 to 0.00390625
- offsets: int32 [8, 2], P('src'), may hold values from -8 to 7
- material: int32 [6, 2048, 2048], P(None, 'tx', 'ty'), may hold values from 0 to 3
- e_field: float32 [3, 6, 2048, 2048], P(None, None, 'tx', 'ty'), may hold values from -6 to 6
- h_field: float32 [3, 6, 2048, 2048], P(None, None, 'tx', 'ty'), may hold values from -6 to 6
Outputs:
- e_out: float32 [3, 6, 2048, 2048], P(None, None, 'tx', 'ty')
- h_out: float32 [3, 6, 2048, 2048], P(None, None, 'tx', 'ty')
All inputs are finite; a program needn't handle non-finite values.
Results may differ from a plain program's by a relative error of at most 0.0003.
Values sent between devices are 32-bit elements; how exact they have to be, the bound alone decides.
A program may use at most 128 MiB of HBM per device.

v0:
```python
import math

import jax
import jax.numpy as jnp
from jax import lax
from jax.sharding import PartitionSpec as P

MX = 512
MY = 512
STEPS = 4
ZINJ = 1


COURANT = 0.5
OMEGA = 0.7
PERMITTIVITY = (1.0, 2.6, 11.9, 2.1)
HIGH = lax.Precision.HIGHEST


def passed_along(block, axis, distance):
    devices = range(lax.axis_size(axis))
    route = [((i - distance) % len(devices), i) for i in devices]
    return lax.ppermute(block, axis, route)


def phase_tables(freqs, positions, length):
    product = jnp.mod(freqs[:, :, None] * positions[None, None, :], length)
    angle = product.astype(jnp.float32) * (2.0 * math.pi / length)
    return (jnp.cos(angle), jnp.sin(angle))


def cell_coefficient(material):
    total = jnp.zeros(material.shape, jnp.float32)
    for number in range(len(PERMITTIVITY)):
        total = total + jnp.where(material == number, COURANT / PERMITTIVITY[number], 0.0)
    return total


def ahead(field, rim, axis):
    following = lax.slice_in_dim(field, 1, field.shape[axis], axis=axis)
    return jnp.concatenate([following, rim], axis) - field


def behind(field, rim, axis):
    earlier = lax.slice_in_dim(field, 0, field.shape[axis] - 1, axis=axis)
    return field - jnp.concatenate([rim, earlier], axis)


def neighbour_rims(row_x, col_y, offset):
    got_x = passed_along(row_x, "tx", offset)
    got_y = passed_along(col_y, "ty", offset)
    return (got_x, got_y)


def per_device(orders, offsets, material, e_field, h_field):
    points, _, rows_kx, cols_ky = orders.shape
    layers, cells_x, cells_y = material.shape
    full_x = cells_x * lax.axis_size("tx")
    full_y = cells_y * lax.axis_size("ty")
    amp_re = orders[:, 0]
    amp_im = orders[:, 1]
    kx_glob = lax.axis_index("tx") * rows_kx + jnp.arange(rows_kx, dtype=jnp.int32)
    ky_own = lax.axis_index("ty") * cols_ky + jnp.arange(cols_ky, dtype=jnp.int32)
    freq_x = kx_glob[None, :] - MX // 2 + offsets[:, 0:1]
    freq_y = ky_own[None, :] - MY // 2 + offsets[:, 1:2]
    y_pos = jnp.arange(cells_y * lax.axis_size("ty"), dtype=jnp.int32)
    cos_y, sin_y = phase_tables(freq_y, y_pos, full_y)
    inner_inner_re = jnp.einsum("pak,pky->ypa", amp_re, cos_y, precision=HIGH) - jnp.einsum(
        "pak,pky->ypa", amp_im, sin_y, precision=HIGH
    )
    inner_inner_im = jnp.einsum("pak,pky->ypa", amp_re, sin_y, precision=HIGH) + jnp.einsum(
        "pak,pky->ypa", amp_im, cos_y, precision=HIGH
    )
    inner = lax.psum_scatter(
        jnp.stack([inner_inner_re, inner_inner_im], 2).reshape(
            cos_y.shape[2], points * 2 * rows_kx
        ),
        "ty",
        scatter_dimension=0,
        tiled=True,
    )
    inner = inner.reshape(cells_y, points, 2, rows_kx)
    inner_re = inner[:, :, 0]
    inner_im = inner[:, :, 1]
    x_pos = jnp.arange(cells_x * lax.axis_size("tx"), dtype=jnp.int32)
    cos_x, sin_x = phase_tables(freq_x, x_pos, full_x)
    plane_re = jnp.einsum("pkx,ypk->xy", cos_x, inner_re, precision=HIGH) - jnp.einsum(
        "pkx,ypk->xy", sin_x, inner_im, precision=HIGH
    )
    plane_im = jnp.einsum("pkx,ypk->xy", cos_x, inner_im, precision=HIGH) + jnp.einsum(
        "pkx,ypk->xy", sin_x, inner_re, precision=HIGH
    )
    partial_plane = lax.psum_scatter(
        jnp.stack([plane_re, plane_im], 1), "tx", scatter_dimension=0, tiled=True
    )
    plane = lax.psum(partial_plane, "src")
    plane_re = plane[:, 0, :]
    plane_im = plane[:, 1, :]
    coefficient = cell_coefficient(material)
    zero_z = jnp.zeros((1, cells_x, cells_y), jnp.float32)
    e_x, e_y, e_z = (e_field[0], e_field[1], e_field[2])
    h_x, h_y, h_z = (h_field[0], h_field[1], h_field[2])
    for step in range(STEPS):
        rim_x, rim_y = neighbour_rims(
            jnp.stack([e_y[:, 0, :], e_z[:, 0, :]]), jnp.stack([e_x[:, :, 0], e_z[:, :, 0]]), -1
        )
        h_x = h_x - COURANT * (ahead(e_z, rim_y[1][:, :, None], 2) - ahead(e_y, zero_z, 0))
        h_y = h_y - COURANT * (ahead(e_x, zero_z, 0) - ahead(e_z, rim_x[1][:, None, :], 1))
        h_z = h_z - COURANT * (
            ahead(e_y, rim_x[0][:, None, :], 1) - ahead(e_x, rim_y[0][:, :, None], 2)
        )
        rim_x, rim_y = neighbour_rims(
            jnp.stack([h_y[:, -1, :], h_z[:, -1, :]]), jnp.stack([h_x[:, :, -1], h_z[:, :, -1]]), 1
        )
        e_x = e_x + coefficient * (behind(h_z, rim_y[1][:, :, None], 2) - behind(h_y, zero_z, 0))
        e_y = e_y + coefficient * (behind(h_x, zero_z, 0) - behind(h_z, rim_x[1][:, None, :], 1))
        e_z = e_z + coefficient * (
            behind(h_y, rim_x[0][:, None, :], 1) - behind(h_x, rim_y[0][:, :, None], 2)
        )
        cosine = math.cos(OMEGA * (step + 1))
        sine = math.sin(OMEGA * (step + 1))
        e_x = e_x.at[ZINJ].add(COURANT * (cosine * plane_re - sine * plane_im))
        e_y = e_y.at[ZINJ].add(COURANT * (sine * plane_re + cosine * plane_im))
    return (jnp.stack([e_x, e_y, e_z]), jnp.stack([h_x, h_y, h_z]))


def solution(mesh):
    in_specs = (
        P("src", None, "tx", "ty"),
        P("src", None),
        P(None, "tx", "ty"),
        P(None, None, "tx", "ty"),
        P(None, None, "tx", "ty"),
    )
    out_specs = (P(None, None, "tx", "ty"), P(None, None, "tx", "ty"))
    return jax.shard_map(
        per_device, mesh=mesh, in_specs=in_specs, out_specs=out_specs, check_vma=False
    )
```

profile of v0, /device:TPU:1, one launch (start us, length us, event | category | flops | bytes accessed | tf_op | source)
XLA Modules:
  0.0 378.7 jit_solution(12795948664375831719)
XLA Ops:
  8.1 7.2 %fusion.102 = f32[4,2048,64]{1,2,0:T(8,128)S(1)} fusion(s32[4,32]{1,0:T(4,128)S(1)} %broadcast_add_fusion, f32[4,2,64,32]{2,3,1,0:T(8,128)} %param.21), kind=kOutput, calls=%fused_computation.166 | convolution fusion | flops 204996608 | bytes 2163200 | tf_op jit(solution)/shard_map/pak,pky->ypa/dot_general | solution.py:71
  15.3 6.4 %fusion.100 = f32[4,2048,64]{1,2,0:T(8,128)S(1)} fusion(s32[4,32]{1,0:T(4,128)S(1)} %broadcast_add_fusion, f32[4,2,64,32]{2,3,1,0:T(8,128)S(1)} %copy-done.26), kind=kOutput, calls=%fused_computation.165 | convolution fusion | flops 204996608 | bytes 2164736 | tf_op jit(solution)/shard_map/pak,pky->ypa/dot_general | solution.py:68
  21.7 6.5 %fusion = f32[2048,4,1,64]{0,3,1,2:T(8,128)S(1)} fusion(f32[4,2048,64]{1,2,0:T(8,128)S(1)} %fusion.102, s32[4,32]{1,0:T(4,128)S(1)} %broadcast_add_fusion, f32[4,2,64,32]{2,3,1,0:T(8,128)S(1)} %copy-done.26), kind=kOutput, calls=%fused_computation.5 | convolution fusion | flops 205520896 | bytes 4261888 | tf_op jit(solution)/shard_map/pak,pky->ypa/dot_general | solution.py:71
  28.2 6.5 %fusion.1 = f32[2048,4,1,64]{0,3,1,2:T(8,128)S(1)} fusion(f32[4,2048,64]{1,2,0:T(8,128)S(1)} %fusion.100, s32[4,32]{1,0:T(4,128)S(1)} %broadcast_add_fusion, f32[4,2,64,32]{2,3,1,0:T(8,128)S(1)} %copy-done.26), kind=kOutput, calls=%fused_computation.7 | convolution fusion | flops 205520896 | bytes 4261888 | tf_op jit(solution)/shard_map/pak,pky->ypa/dot_general | solution.py:68
  35.2 2.2 copy.195
  38.1 62.9 %reduce-scatter.3.cloned.1.call-done = f32[128,512]{0,1:T(8,128)} async-done(((f32[2048,512]{0,1:T(8,128)}), f32[128,512]{0,1:T(8,128)}) %reduce-scatter.3.cloned.1.call-update) | async-done | bytes 262160 | tf_op jit(solution)/shard_map/reduce_scatter | solution.py:74
  100.9 11.8 %convolution_bitcast_fusion = f32[2048,128]{1,0:T(8,128)S(1)} fusion(s32[4,64]{1,0:T(4,128)S(1)} %broadcast_add_fusion.1, f32[128,4,2,64]{0,3,2,1:T(8,128)} %bitcast.259), kind=kOutput, calls=%fused_computation.8 | convolution fusion | flops 812646400 | bytes 1180672 | tf_op jit(solution)/shard_map/pkx,ypk->xy/dot_general | solution.py:90
  112.7 11.0 %convolution_bitcast_fusion.2 = f32[2048,128]{1,0:T(8,128)S(1)} fusion(s32[4,64]{1,0:T(4,128)S(1)} %broadcast_add_fusion.1, f32[128,4,2,64]{0,3,2,1:T(8,128)S(1)} %bitcast.260), kind=kOutput, calls=%fused_computation.10 | convolution fusion | flops 812646400 | bytes 1181696 | tf_op jit(solution)/shard_map/pkx,ypk->xy/dot_general | solution.py:87
  123.7 11.0 %fusion.5 = f32[2048,1,128]{2,0,1:T(8,128)S(1)} fusion(f32[2048,128]{1,0:T(8,128)S(1)} %convolution_bitcast_fusion, s32[4,64]{1,0:T(4,128)S(1)} %broadcast_add_fusion.1, f32[128,4,2,64]{0,3,2,1:T(8,128)S(1)} %bitcast.261), kind=kOutput, calls=%fused_computation.15 | convolution fusion | flops 812908544 | bytes 2230272 | tf_op jit(solution)/shard_map/pkx,ypk->xy/dot_general | solution.py:90
  134.8 11.2 %fusion.3 = f32[2048,1,128]{2,0,1:T(8,128)S(1)} fusion(f32[2048,128]{1,0:T(8,128)S(1)} %convolution_bitcast_fusion.2, s32[4,64]{1,0:T(4,128)S(1)} %broadcast_add_fusion.1, f32[128,4,2,64]{0,3,2,1:T(8,128)S(1)} %bitcast.262), kind=kOutput, calls=%fused_computation.13 | convolution fusion | flops 812908544 | bytes 2230272 | tf_op jit(solution)/shard_map/pkx,ypk->xy/dot_general | solution.py:87
  146.0 1.5 pad_maximum_fusion.3
  148.7 5.2 %collective-permute-start = (f32[2,6,128]{2,0,1:T(2,128)S(1)}, f32[2,6,128]{2,0,1:T(2,128)S(1)}, u32[]{:S(2)}, u32[]{:S(2)}) collective-permute-start(f32[2,6,128]{2,0,1:T(2,128)S(1)} %pad_maximum_fusion.12), channel_id=1, source_target_pairs={{16,0},{32,16},{48,32},{64,48},{80,64},{96,80},{112,96},{0,112},{1... | collective-permute-start | bytes 18440 | tf_op jit(solution)/shard_map/ppermute | solution.py:23
  154.4 4.0 %collective-permute-start.1 = (f32[2,6,256]{2,0,1:T(2,128)S(1)}, f32[2,6,256]{2,0,1:T(2,128)S(1)}, u32[]{:S(2)}, u32[]{:S(2)}) collective-permute-start(f32[2,6,256]{2,0,1:T(2,128)S(1)} %pad_maximum_fusion.4), channel_id=1, source_target_pairs={{1,0},{2,1},{3,2},{4,3},{5,4},{6,5},{7,6},{8,7},{9,8},{10,9},{11,1... | collective-permute-start | bytes 36872 | tf_op jit(solution)/shard_map/ppermute | solution.py:23
  158.4 1.2 slice_bitcast_fusion.4
  160.6 1.2 slice.708
  162.7 1.2 slice.712
  163.9 1.2 copy.191
  165.1 1.2 copy.190
  166.3 4.4 %fusion.29 = (f32[6,256,128]{2,1,0:T(8,128)S(1)}, f32[6,256,128]{2,1,0:T(8,128)S(1)}, f32[6,256,128]{2,1,0:T(8,128)S(1)}) fusion(f32[6,256,1]{2,1,0:T(8,128)} %copy.191, f32[6,256,127]{2,1,0:T(8,128)} %slice.712, f32[5,256,128]{2,1,0:T(8,128)} %get-tuple-element.104, f32[3,6,256,128]{3,2,1,0:T(8,128)} %param.25, f32[3,6,256,128]{3,2,1,0:T(8,128)S(1)} %copy-done, ...), kind=kLoop, calls=%fused_computation.60 | loop fusion | flops 3735552 | bytes 11534336 | tf_op jit(solution)/shard_map/sub | solution.py:107
  173.7 4.3 %collective-permute-done.3 = f32[2,6,128]{2,0,1:T(2,128)S(1)} collective-permute-done((f32[2,6,128]{2,0,1:T(2,128)S(1)}, f32[2,6,128]{2,0,1:T(2,128)S(1)}, u32[]{:S(2)}, u32[]{:S(2)}) %collective-permute-start.3) | collective-permute-done | bytes 6176 | tf_op jit(solution)/shard_map/ppermute | solution.py:23
  178.0 1.2 copy.192
  179.2 1.2 copy.198
  180.4 6.0 %fusion.32 = (f32[6,256,128]{2,1,0:T(8,128)}, f32[6,256,128]{2,1,0:T(8,128)S(1)}, f32[6,256,128]{2,1,0:T(8,128)}) fusion(f32[6,256,128]{2,1,0:T(8,128)} %copy-done.1, f32[6,256,127]{2,1,0:T(8,128)} %bitcast.237, f32[6,256,1]{2,1,0:T(8,128)} %copy.192, f32[6,256,128]{2,1,0:T(8,128)} %copy-done.20, f32[5,256,128]{2,1,0:T(8,128)} %slice.720, ...), kind=kLoop, calls=%fused_computation.64 | loop fusion | flops 5898240 | bytes 12320768 | tf_op jit(solution)/shard_map/add | solution.py:115
  186.4 42.0 %reduce-scatter.5.cloned.1.call-done = f32[256,2,128]{2,0,1:T(8,128)} async-done(((f32[2048,2,128]{2,0,1:T(8,128)}), f32[256,2,128]{2,0,1:T(8,128)}) %reduce-scatter.5.cloned.1.call-update) | async-done | bytes 262160 | tf_op jit(solution)/shard_map/reduce_scatter | solution.py:93
  229.6 1.2 slice.744
  230.7 35.2 %all-reduce.18.cloned.1.call-done = f32[256,2,128]{2,0,1:T(8,128)} async-done(((f32[256,2,128]{2,0,1:T(8,128)}), f32[256,2,128]{2,0,1:T(8,128)}) %all-reduce.18.cloned.1.call-update) | async-done | bytes 262160 | tf_op jit(solution)/shard_map/psum | solution.py:96
  266.0 1.0 fusion.114
  267.3 4.6 %collective-permute-start.4 = (f32[2,6,128]{2,0,1:T(2,128)S(1)}, f32[2,6,128]{2,0,1:T(2,128)S(1)}, u32[]{:S(2)}, u32[]{:S(2)}) collective-permute-start(f32[2,6,128]{2,0,1:T(2,128)S(1)} %pad_maximum_fusion.14), channel_id=1, source_target_pairs={{16,0},{32,16},{48,32},{64,48},{80,64},{96,80},{112,96},{0,112},{1... | collective-permute-start | bytes 18440 | tf_op jit(solution)/shard_map/ppermute | solution.py:23
  273.9 1.2 slice.740
  276.0 1.4 collective-permute-start.5
  277.4 2.5 collective-permute-done.5
  279.9 1.2 copy.200
  281.1 1.2 copy.199
  282.4 4.3 %fusion.47 = (f32[6,256,128]{2,1,0:T(8,128)S(1)}, f32[6,256,128]{2,1,0:T(8,128)S(1)}, f32[6,256,128]{2,1,0:T(8,128)S(1)}) fusion(f32[6,256,128]{2,1,0:T(8,128)} %copy-done.11, f32[6,256,128]{2,1,0:T(8,128)S(1)} %get-tuple-element.102, f32[6,256,1]{2,1,0:T(8,128)} %copy.200, f32[6,256,127]{2,1,0:T(8,128)} %slice.744, f32[6,256,128]{2,1,0:T(8,128)} %copy-done.17, ...), kind=kLoop, calls=%fused_computation.86 | loop fusion | flops 3735552 | bytes 11534336 | tf_op jit(solution)/shard_map/sub | solution.py:107
  290.0 4.2 %collective-permute-done.7 = f32[2,6,128]{2,0,1:T(2,128)S(1)} collective-permute-done((f32[2,6,128]{2,0,1:T(2,128)S(1)}, f32[2,6,128]{2,0,1:T(2,128)S(1)}, u32[]{:S(2)}, u32[]{:S(2)}) %collective-permute-start.7) | collective-permute-done | bytes 6176 | tf_op jit(solution)/shard_map/ppermute | solution.py:23
  294.2 1.2 copy.201
  295.4 1.2 copy.202
  296.6 4.2 %fusion.50 = (f32[6,256,128]{2,1,0:T(8,128)S(1)}, f32[6,256,128]{2,1,0:T(8,128)S(1)}, f32[6,256,128]{2,1,0:T(8,128)S(1)}) fusion(f32[6,256,128]{2,1,0:T(8,128)S(1)} %copy-done.5, f32[6,256,128]{2,1,0:T(8,128)S(1)} %get-tuple-element.125, f32[6,256,127]{2,1,0:T(8,128)S(1)} %bitcast.239, f32[6,256,1]{2,1,0:T(8,128)} %copy.201, f32[6,256,128]{2,1,0:T(8,128)} %copy-done.21, ...), kind=kLoop, calls=%fused_computation.90 | loop fusion | flops 5898240 | bytes 12320768 | tf_op jit(solution)/shard_map/add | solution.py:115
  301.6 2.7 collective-permute-start.8
  306.1 1.2 slice.770
  307.2 1.0 slice.762
  309.2 1.2 slice.774
  310.4 3.9 %collective-permute-start.9 = (f32[2,6,256]{2,0,1:T(2,128)S(1)}, f32[2,6,256]{2,0,1:T(2,128)S(1)}, u32[]{:S(2)}, u32[]{:S(2)}) collective-permute-start(f32[2,6,256]{2,0,1:T(2,128)S(1)} %pad_maximum_fusion.8), channel_id=1, source_target_pairs={{1,0},{2,1},{3,2},{4,3},{5,4},{6,5},{7,6},{8,7},{9,8},{10,9},{11,1... | collective-permute-start | bytes 36872 | tf_op jit(solution)/shard_map/ppermute | solution.py:23
  315.1 1.2 copy.204
  316.3 1.2 copy.203
  317.5 4.3 %fusion.65 = (f32[6,256,128]{2,1,0:T(8,128)S(1)}, f32[6,256,128]{2,1,0:T(8,128)S(1)}, f32[6,256,128]{2,1,0:T(8,128)S(1)}) fusion(f32[6,256,128]{2,1,0:T(8,128)} %copy-done.12, f32[6,256,128]{2,1,0:T(8,128)S(1)} %get-tuple-element.116, f32[6,256,1]{2,1,0:T(8,128)} %copy.204, f32[6,256,127]{2,1,0:T(8,128)} %slice.774, f32[6,256,128]{2,1,0:T(8,128)} %copy-done.18, ...), kind=kLoop, calls=%fused_computation.112 | loop fusion | flops 3735552 | bytes 11534336 | tf_op jit(solution)/shard_map/sub | solution.py:107
  324.9 4.3 %collective-permute-done.11 = f32[2,6,128]{2,0,1:T(2,128)S(1)} collective-permute-done((f32[2,6,128]{2,0,1:T(2,128)S(1)}, f32[2,6,128]{2,0,1:T(2,128)S(1)}, u32[]{:S(2)}, u32[]{:S(2)}) %collective-permute-start.11) | collective-permute-done | bytes 6176 | tf_op jit(solution)/shard_map/ppermute | solution.py:23
  329.2 1.2 copy.205
  330.4 1.2 copy.206
  331.5 4.2 %fusion.68 = (f32[6,256,128]{2,1,0:T(8,128)S(1)}, f32[6,256,128]{2,1,0:T(8,128)S(1)}, f32[6,256,128]{2,1,0:T(8,128)S(1)}) fusion(f32[6,256,128]{2,1,0:T(8,128)S(1)} %copy-done.8, f32[6,256,128]{2,1,0:T(8,128)S(1)} %get-tuple-element.122, f32[6,256,127]{2,1,0:T(8,128)S(1)} %bitcast.241, f32[6,256,1]{2,1,0:T(8,128)} %copy.205, f32[6,256,128]{2,1,0:T(8,128)} %copy-done.22, ...), kind=kLoop, calls=%fused_computation.116 | loop fusion | flops 5898240 | bytes 12320768 | tf_op jit(solution)/shard_map/add | solution.py:115
  336.5 2.6 collective-permute-start.12
  341.0 1.2 slice.800
  342.1 1.0 slice.792
  344.0 1.2 slice.804
  345.2 3.9 %collective-permute-start.13 = (f32[2,6,256]{2,0,1:T(2,128)S(1)}, f32[2,6,256]{2,0,1:T(2,128)S(1)}, u32[]{:S(2)}, u32[]{:S(2)}) collective-permute-start(f32[2,6,256]{2,0,1:T(2,128)S(1)} %pad_maximum_fusion.10), channel_id=1, source_target_pairs={{1,0},{2,1},{3,2},{4,3},{5,4},{6,5},{7,6},{8,7},{9,8},{10,9},{11,1... | collective-permute-start | bytes 36872 | tf_op jit(solution)/shard_map/ppermute | solution.py:23
  350.0 1.2 copy.208
  351.2 1.2 copy.207
  352.4 4.3 %fusion.83 = (f32[6,256,128]{2,1,0:T(8,128)S(1)}, f32[6,256,128]{2,1,0:T(8,128)S(1)}, f32[6,256,128]{2,1,0:T(8,128)S(1)}) fusion(f32[6,256,128]{2,1,0:T(8,128)} %copy-done.13, f32[6,256,128]{2,1,0:T(8,128)S(1)} %get-tuple-element.113, f32[6,256,1]{2,1,0:T(8,128)} %copy.208, f32[6,256,127]{2,1,0:T(8,128)} %slice.804, f32[6,256,128]{2,1,0:T(8,128)} %copy-done.19, ...), kind=kLoop, calls=%fused_computation.138 | loop fusion | flops 3735552 | bytes 11534336 | tf_op jit(solution)/shard_map/sub | solution.py:107
  357.9 1.6 pad_maximum_fusion.2
  361.3 2.7 collective-permute-done.15
  364.0 1.2 copy.209
  365.2 1.2 copy.210
  366.4 3.7 fusion.86
  370.3 1.6 pad_maximum_fusion.1
  (189 shorter events, 30.7 us)
Async XLA Ops:
  7.2 93.8 %reduce-scatter.3.cloned.1.call-start = ((), (), s32[]{:S(2)}) async-start(), calls=%async_computation.2 | async-start | bytes 4456448 | tf_op jit(solution)/shard_map/reduce_scatter | solution.py:74
  8.1 7.2 %copy-start.26 = (f32[4,2,64,32]{2,3,1,0:T(8,128)S(1)}, f32[4,2,64,32]{2,3,1,0:T(8,128)}, u32[]{:S(2)}) copy-start(f32[4,2,64,32]{2,3,1,0:T(8,128)} %param.21) | copy-start | bytes 196612
  37.4 190.9 %reduce-scatter.5.cloned.1.call-start = ((), (), s32[]{:S(2)}) async-start(), calls=%async_computation.3 | async-start | bytes 2359296 | tf_op jit(solution)/shard_map/reduce_scatter | solution.py:93
  100.9 11.8 %copy-start.25 = (f32[128,512]{0,1:T(8,128)S(1)}, f32[128,512]{0,1:T(8,128)}, u32[]{:S(2)}) copy-start(f32[128,512]{0,1:T(8,128)} %reduce-scatter.3.cloned.1.call-done) | copy-start | bytes 786436
  146.0 2.4 copy-start
  147.5 118.4 %all-reduce.18.cloned.1.call-start = ((), (), s32[]{:S(2)}) async-start(), calls=%async_computation.4 | async-start | bytes 524288 | tf_op jit(solution)/shard_map/psum | solution.py:96
  148.7 15.2 %collective-permute-start = (f32[2,6,128]{2,0,1:T(2,128)S(1)}, f32[2,6,128]{2,0,1:T(2,128)S(1)}, u32[]{:S(2)}, u32[]{:S(2)}) collective-permute-start(f32[2,6,128]{2,0,1:T(2,128)S(1)} %pad_maximum_fusion.12), channel_id=1, source_target_pairs={{16,0},{32,16},{48,32},{64,48},{80,64},{96,80},{112,96},{0,112},{1... | collective-permute-start | bytes 18440 | tf_op jit(solution)/shard_map/ppermute | solution.py:23
  154.4 9.5 %collective-permute-start.1 = (f32[2,6,256]{2,0,1:T(2,128)S(1)}, f32[2,6,256]{2,0,1:T(2,128)S(1)}, u32[]{:S(2)}, u32[]{:S(2)}) collective-permute-start(f32[2,6,256]{2,0,1:T(2,128)S(1)} %pad_maximum_fusion.4), channel_id=1, source_target_pairs={{1,0},{2,1},{3,2},{4,3},{5,4},{6,5},{7,6},{8,7},{9,8},{10,9},{11,1... | collective-permute-start | bytes 36872 | tf_op jit(solution)/shard_map/ppermute | solution.py:23
  170.7 3.0 copy-start.1
  170.7 3.0 copy-start.20
  170.7 3.0 copy-start.11
  171.8 6.2 %collective-permute-start.3 = (f32[2,6,128]{2,0,1:T(2,128)S(1)}, f32[2,6,128]{2,0,1:T(2,128)S(1)}, u32[]{:S(2)}, u32[]{:S(2)}) collective-permute-start(f32[2,6,128]{2,0,1:T(2,128)S(1)} %pad_maximum_fusion.13), channel_id=1, source_target_pairs={{112,0},{0,16},{16,32},{32,48},{48,64},{64,80},{80,96},{96,112},{1... | collective-permute-start | bytes 18440 | tf_op jit(solution)/shard_map/ppermute | solution.py:23
  173.7 4.3 %collective-permute-start.2 = (f32[2,6,256]{2,0,1:T(2,128)S(1)}, f32[2,6,256]{2,0,1:T(2,128)S(1)}, u32[]{:S(2)}, u32[]{:S(2)}) collective-permute-start(f32[2,6,256]{2,0,1:T(2,128)S(1)} %pad_maximum_fusion.5), channel_id=1, source_target_pairs={{15,0},{0,1},{1,2},{2,3},{3,4},{4,5},{5,6},{6,7},{7,8},{8,9},{9,10... | collective-permute-start | bytes 36872 | tf_op jit(solution)/shard_map/ppermute | solution.py:23
  228.3 37.6 %copy-start.3 = (f32[6,256,128]{2,1,0:T(8,128)S(1)}, f32[6,256,128]{2,1,0:T(8,128)}, u32[]{:S(2)}) copy-start(f32[6,256,128]{2,1,0:T(8,128)} %get-tuple-element.101) | copy-start | bytes 2359300
  228.3 37.6 %copy-start.16 = (f32[6,256,128]{2,1,0:T(8,128)S(1)}, f32[6,256,128]{2,1,0:T(8,128)}, u32[]{:S(2)}) copy-start(f32[6,256,128]{2,1,0:T(8,128)} %get-tuple-element.103) | copy-start | bytes 2359300
  267.0 8.0 %copy-start.17 = (f32[6,256,128]{2,1,0:T(8,128)}, f32[6,256,128]{2,1,0:T(8,128)S(1)}, u32[]{:S(2)}) copy-start(f32[6,256,128]{2,1,0:T(8,128)S(1)} %get-tuple-element.134) | copy-start | bytes 2359300
  267.0 15.4 %copy-start.4 = (f32[6,256,128]{2,1,0:T(8,128)}, f32[6,256,128]{2,1,0:T(8,128)S(1)}, u32[]{:S(2)}) copy-start(f32[6,256,128]{2,1,0:T(8,128)S(1)} %get-tuple-element.133) | copy-start | bytes 2359300
  267.3 10.1 %collective-permute-start.4 = (f32[2,6,128]{2,0,1:T(2,128)S(1)}, f32[2,6,128]{2,0,1:T(2,128)S(1)}, u32[]{:S(2)}, u32[]{:S(2)}) collective-permute-start(f32[2,6,128]{2,0,1:T(2,128)S(1)} %pad_maximum_fusion.14), channel_id=1, source_target_pairs={{16,0},{32,16},{48,32},{64,48},{80,64},{96,80},{112,96},{0,112},{1... | collective-permute-start | bytes 18440 | tf_op jit(solution)/shard_map/ppermute | solution.py:23
  273.9 8.5 %copy-start.2 = (f32[6,256,128]{2,1,0:T(8,128)S(1)}, f32[6,256,128]{2,1,0:T(8,128)}, u32[]{:S(2)}) copy-start(f32[6,256,128]{2,1,0:T(8,128)} %copy-done.1) | copy-start | bytes 2359300
  276.0 3.9 %collective-permute-start.5 = (f32[2,6,256]{2,0,1:T(2,128)S(1)}, f32[2,6,256]{2,0,1:T(2,128)S(1)}, u32[]{:S(2)}, u32[]{:S(2)}) collective-permute-start(f32[2,6,256]{2,0,1:T(2,128)S(1)} %pad_maximum_fusion.6), channel_id=1, source_target_pairs={{1,0},{2,1},{3,2},{4,3},{5,4},{6,5},{7,6},{8,7},{9,8},{10,9},{11,1... | collective-permute-start | bytes 36872 | tf_op jit(solution)/shard_map/ppermute | solution.py:23
  286.7 1.4 copy-start.12
  286.7 3.2 copy-start.21
  287.8 6.4 %collective-permute-start.7 = (f32[2,6,128]{2,0,1:T(2,128)S(1)}, f32[2,6,128]{2,0,1:T(2,128)S(1)}, u32[]{:S(2)}, u32[]{:S(2)}) collective-permute-start(f32[2,6,128]{2,0,1:T(2,128)S(1)} %pad_maximum_fusion.15), channel_id=1, source_target_pairs={{112,0},{0,16},{16,32},{32,48},{48,64},{64,80},{80,96},{96,112},{1... | collective-permute-start | bytes 18440 | tf_op jit(solution)/shard_map/ppermute | solution.py:23
  288.2 8.5 %copy-start.5 = (f32[6,256,128]{2,1,0:T(8,128)S(1)}, f32[6,256,128]{2,1,0:T(8,128)}, u32[]{:S(2)}) copy-start(f32[6,256,128]{2,1,0:T(8,128)} %copy-done.4) | copy-start | bytes 2359300
  289.9 4.3 %collective-permute-start.6 = (f32[2,6,256]{2,0,1:T(2,128)S(1)}, f32[2,6,256]{2,0,1:T(2,128)S(1)}, u32[]{:S(2)}, u32[]{:S(2)}) collective-permute-start(f32[2,6,256]{2,0,1:T(2,128)S(1)} %pad_maximum_fusion.7), channel_id=1, source_target_pairs={{15,0},{0,1},{1,2},{2,3},{3,4},{4,5},{5,6},{6,7},{7,8},{8,9},{9,10... | collective-permute-start | bytes 36872 | tf_op jit(solution)/shard_map/ppermute | solution.py:23
  296.6 4.5 %copy-start.24 = (f32[256,2,128]{2,0,1:T(8,128)S(1)}, f32[256,2,128]{2,0,1:T(8,128)}, u32[]{:S(2)}) copy-start(f32[256,2,128]{2,0,1:T(8,128)} %all-reduce.18.cloned.1.call-done) | copy-start | bytes 786436
  301.2 6.0 %copy-start.6 = (f32[6,256,128]{2,1,0:T(8,128)}, f32[6,256,128]{2,1,0:T(8,128)S(1)}, u32[]{:S(2)}) copy-start(f32[6,256,128]{2,1,0:T(8,128)S(1)} %get-tuple-element.131) | copy-start | bytes 2359300
  301.3 6.0 %copy-start.18 = (f32[6,256,128]{2,1,0:T(8,128)}, f32[6,256,128]{2,1,0:T(8,128)S(1)}, u32[]{:S(2)}) copy-start(f32[6,256,128]{2,1,0:T(8,128)S(1)} %get-tuple-element.132) | copy-start | bytes 2359300
  301.6 12.7 %collective-permute-start.8 = (f32[2,6,128]{2,0,1:T(2,128)S(1)}, f32[2,6,128]{2,0,1:T(2,128)S(1)}, u32[]{:S(2)}, u32[]{:S(2)}) collective-permute-start(f32[2,6,128]{2,0,1:T(2,128)S(1)} %pad_maximum_fusion.16), channel_id=1, source_target_pairs={{16,0},{32,16},{48,32},{64,48},{80,64},{96,80},{112,96},{0,112},{1... | collective-permute-start | bytes 18440 | tf_op jit(solution)/shard_map/ppermute | solution.py:23
  308.2 9.3 %copy-start.7 = (f32[6,256,128]{2,1,0:T(8,128)S(1)}, f32[6,256,128]{2,1,0:T(8,128)}, u32[]{:S(2)}) copy-start(f32[6,256,128]{2,1,0:T(8,128)} %copy-done.6) | copy-start | bytes 2359300
  310.4 4.8 %collective-permute-start.9 = (f32[2,6,256]{2,0,1:T(2,128)S(1)}, f32[2,6,256]{2,0,1:T(2,128)S(1)}, u32[]{:S(2)}, u32[]{:S(2)}) collective-permute-start(f32[2,6,256]{2,0,1:T(2,128)S(1)} %pad_maximum_fusion.8), channel_id=1, source_target_pairs={{1,0},{2,1},{3,2},{4,3},{5,4},{6,5},{7,6},{8,7},{9,8},{10,9},{11,1... | collective-permute-start | bytes 36872 | tf_op jit(solution)/shard_map/ppermute | solution.py:23
  321.9 1.2 copy-start.13
  321.9 3.0 copy-start.22
  323.0 6.2 %collective-permute-start.11 = (f32[2,6,128]{2,0,1:T(2,128)S(1)}, f32[2,6,128]{2,0,1:T(2,128)S(1)}, u32[]{:S(2)}, u32[]{:S(2)}) collective-permute-start(f32[2,6,128]{2,0,1:T(2,128)S(1)} %pad_maximum_fusion.17), channel_id=1, source_target_pairs={{112,0},{0,16},{16,32},{32,48},{48,64},{64,80},{80,96},{96,112},{1... | collective-permute-start | bytes 18440 | tf_op jit(solution)/shard_map/ppermute | solution.py:23
  323.1 8.5 %copy-start.8 = (f32[6,256,128]{2,1,0:T(8,128)S(1)}, f32[6,256,128]{2,1,0:T(8,128)}, u32[]{:S(2)}) copy-start(f32[6,256,128]{2,1,0:T(8,128)} %copy-done.6) | copy-start | bytes 2359300
  324.9 4.3 %collective-permute-start.10 = (f32[2,6,256]{2,0,1:T(2,128)S(1)}, f32[2,6,256]{2,0,1:T(2,128)S(1)}, u32[]{:S(2)}, u32[]{:S(2)}) collective-permute-start(f32[2,6,256]{2,0,1:T(2,128)S(1)} %pad_maximum_fusion.9), channel_id=1, source_target_pairs={{15,0},{0,1},{1,2},{2,3},{3,4},{4,5},{5,6},{6,7},{7,8},{8,9},{9,10... | collective-permute-start | bytes 36872 | tf_op jit(solution)/shard_map/ppermute | solution.py:23
  336.2 5.9 %copy-start.9 = (f32[6,256,128]{2,1,0:T(8,128)}, f32[6,256,128]{2,1,0:T(8,128)S(1)}, u32[]{:S(2)}) copy-start(f32[6,256,128]{2,1,0:T(8,128)S(1)} %get-tuple-element.129) | copy-start | bytes 2359300
  336.2 5.9 %copy-start.19 = (f32[6,256,128]{2,1,0:T(8,128)}, f32[6,256,128]{2,1,0:T(8,128)S(1)}, u32[]{:S(2)}) copy-start(f32[6,256,128]{2,1,0:T(8,128)S(1)} %get-tuple-element.130) | copy-start | bytes 2359300
  336.5 12.6 %collective-permute-start.12 = (f32[2,6,128]{2,0,1:T(2,128)S(1)}, f32[2,6,128]{2,0,1:T(2,128)S(1)}, u32[]{:S(2)}, u32[]{:S(2)}) collective-permute-start(f32[2,6,128]{2,0,1:T(2,128)S(1)} %pad_maximum_fusion.18), channel_id=1, source_target_pairs={{16,0},{32,16},{48,32},{64,48},{80,64},{96,80},{112,96},{0,112},{1... | collective-permute-start | bytes 18440 | tf_op jit(solution)/shard_map/ppermute | solution.py:23
  343.1 9.3 %copy-start.10 = (f32[6,256,128]{2,1,0:T(8,128)S(1)}, f32[6,256,128]{2,1,0:T(8,128)}, u32[]{:S(2)}) copy-start(f32[6,256,128]{2,1,0:T(8,128)} %copy-done.9) | copy-start | bytes 2359300
  345.2 4.8 %collective-permute-start.13 = (f32[2,6,256]{2,0,1:T(2,128)S(1)}, f32[2,6,256]{2,0,1:T(2,128)S(1)}, u32[]{:S(2)}, u32[]{:S(2)}) collective-permute-start(f32[2,6,256]{2,0,1:T(2,128)S(1)} %pad_maximum_fusion.10), channel_id=1, source_target_pairs={{1,0},{2,1},{3,2},{4,3},{5,4},{6,5},{7,6},{8,7},{9,8},{10,9},{11,1... | collective-permute-start | bytes 36872 | tf_op jit(solution)/shard_map/ppermute | solution.py:23
  356.7 2.8 copy-start.14
  356.7 3.7 copy-start.23
  357.8 6.2 %collective-permute-start.15 = (f32[2,6,128]{2,0,1:T(2,128)S(1)}, f32[2,6,128]{2,0,1:T(2,128)S(1)}, u32[]{:S(2)}, u32[]{:S(2)}) collective-permute-start(f32[2,6,128]{2,0,1:T(2,128)S(1)} %pad_maximum_fusion.19), channel_id=1, source_target_pairs={{112,0},{0,16},{16,32},{32,48},{48,64},{64,80},{80,96},{96,112},{1... | collective-permute-start | bytes 18440 | tf_op jit(solution)/shard_map/ppermute | solution.py:23
  360.4 6.0 %copy-start.15 = (f32[6,256,128]{2,1,0:T(8,128)S(1)}, f32[6,256,128]{2,1,0:T(8,128)}, u32[]{:S(2)}) copy-start(f32[6,256,128]{2,1,0:T(8,128)} %copy-done.14) | copy-start | bytes 2359300
  361.3 2.7 collective-permute-start.14
Sparse Core Ops, SparseCore 0:
  37.5 63.3 reduce-scatter.2
  147.6 80.6 reduce-scatter.4
  231.1 34.8 all-reduce.17
where the time goes:
time: 386 us; the launch traced here: 379 us
  waiting for transfers between devices  160 us (41%)
  matrix products  71.6 us (19%)
  local copies, waits for them, and re-layouts  60.5 us (16%)
  other arithmetic  42.3 us (11%)
  starting transfers between devices  29.7 us (8%)
  between operations  14.9 us (4%)
    reduce_scatter x1, waiting for transfers between devices, per_device(): lax.psum_scatter(jnp.stack([inner_inner_re, inner_inner_im], 2).reshape(c...  62.9 us
    reduce_scatter x1, waiting for transfers between devices, per_device(): lax.psum_scatter(jnp.stack([plane_re, plane_im], 1), 'tx', scatter_dimens...  42 us
    psum x1, waiting for transfers between devices, per_device(): plane = lax.psum(partial_plane, 'src')  35.2 us
    ppermute x16, starting transfers between devices, passed_along(): return lax.ppermute(block, axis, route)  29 us
    slice x23, local copies, waits for them, and re-layouts, ahead(): following = lax.slice_in_dim(field, 1, field.shape[axis], axis=axis)  23.6 us
    ppermute x16, waiting for transfers between devices, passed_along(): return lax.ppermute(block, axis, route)  19.6 us
    add x4, other arithmetic, per_device(): e_x + coefficient * (behind(h_z, rim_y[1][:, :, None], 2) - behind(h_y, z...  18.2 us
    sub x4, other arithmetic, per_device(): h_x - COURANT * (ahead(e_z, rim_y[1][:, :, None], 2) - ahead(e_y, zero_z,...  17.4 us
  transfers between devices with their start and end apart: 19, of which 10 were waited for; matrix products, arithmetic and copies ran while one was open for 13% of the time, Pallas kernels for 0%

commit v1 on v0

v1 whole, which is shorter than its diff:
```python
import math

import jax
import jax.numpy as jnp
from jax import lax
from jax.sharding import PartitionSpec as P

STEPS = 4
ZINJ = 1


COURANT = 0.5
OMEGA = 0.7
PERMITTIVITY = (1.0, 2.6, 11.9, 2.1)
PREC = lax.Precision.HIGH
SPLIT = 32


def passed_along(block, axis, distance):
    devices = range(lax.axis_size(axis))
    route = [((i - distance) % len(devices), i) for i in devices]
    return lax.ppermute(block, axis, route)


def phase_tables(freqs, positions, length):
    product = jnp.mod(freqs[:, None] * positions[None, :], length)
    angle = product.astype(jnp.float32) * (2.0 * math.pi / length)
    return (jnp.cos(angle), jnp.sin(angle))


def base_tables(orders_n, positions, length):
    hi = jnp.arange(orders_n // SPLIT, dtype=jnp.int32) * SPLIT
    lo = jnp.arange(SPLIT, dtype=jnp.int32) - orders_n // 2
    c1, s1 = phase_tables(hi, positions, length)
    c2, s2 = phase_tables(lo, positions, length)
    cos_t = c1[:, None, :] * c2[None, :, :] - s1[:, None, :] * s2[None, :, :]
    sin_t = s1[:, None, :] * c2[None, :, :] + c1[:, None, :] * s2[None, :, :]
    return cos_t.reshape(orders_n, -1), sin_t.reshape(orders_n, -1)


def cell_coefficient(material):
    total = jnp.zeros(material.shape, jnp.float32)
    for number in range(len(PERMITTIVITY)):
        total = total + jnp.where(material == number, COURANT / PERMITTIVITY[number], 0.0)
    return total


def fwd(field, axis):
    if axis == 0:
        zero = jnp.zeros((1,) + field.shape[1:], jnp.float32)
        return jnp.concatenate([field[1:], zero], 0) - field
    return jnp.roll(field, -1, axis) - field


def bwd(field, axis):
    if axis == 0:
        zero = jnp.zeros((1,) + field.shape[1:], jnp.float32)
        return field - jnp.concatenate([zero, field[:-1]], 0)
    return field - jnp.roll(field, 1, axis)


def injection_plane(orders, offsets, cells_x, cells_y):
    points, _, rows_kx, cols_ky = orders.shape
    n_tx = lax.axis_size("tx")
    n_ty = lax.axis_size("ty")
    full_x = cells_x * n_tx
    full_y = cells_y * n_ty
    mx = rows_kx * n_tx
    my = cols_ky * n_ty
    amp = lax.all_gather(orders, "ty", axis=3, tiled=True)
    a_re = amp[:, 0]
    a_im = amp[:, 1]
    y_pos = lax.axis_index("ty") * cells_y + jnp.arange(cells_y, dtype=jnp.int32)
    by_c, by_s = base_tables(my, y_pos, full_y)
    sy_c, sy_s = phase_tables(offsets[:, 1], y_pos, full_y)
    m_re = jnp.einsum("pkj,jy->pky", a_re, by_c, precision=PREC) - jnp.einsum(
        "pkj,jy->pky", a_im, by_s, precision=PREC
    )
    m_im = jnp.einsum("pkj,jy->pky", a_re, by_s, precision=PREC) + jnp.einsum(
        "pkj,jy->pky", a_im, by_c, precision=PREC
    )
    sy_c = sy_c[:, None, :]
    sy_s = sy_s[:, None, :]
    inner = jnp.stack([m_re * sy_c - m_im * sy_s, m_re * sy_s + m_im * sy_c], 1)
    inner = lax.all_gather(inner, "tx", axis=2, tiled=True)
    i_re = inner[:, 0]
    i_im = inner[:, 1]
    x_pos = lax.axis_index("tx") * cells_x + jnp.arange(cells_x, dtype=jnp.int32)
    bx_c, bx_s = base_tables(mx, x_pos, full_x)
    sx_c, sx_s = phase_tables(offsets[:, 0], x_pos, full_x)
    q_re = jnp.einsum("kx,pky->pxy", bx_c, i_re, precision=PREC) - jnp.einsum(
        "kx,pky->pxy", bx_s, i_im, precision=PREC
    )
    q_im = jnp.einsum("kx,pky->pxy", bx_c, i_im, precision=PREC) + jnp.einsum(
        "kx,pky->pxy", bx_s, i_re, precision=PREC
    )
    sx_c = sx_c[:, :, None]
    sx_s = sx_s[:, :, None]
    plane = jnp.stack(
        [jnp.sum(q_re * sx_c - q_im * sx_s, 0), jnp.sum(q_re * sx_s + q_im * sx_c, 0)]
    )
    return lax.psum(plane, "src")


def with_halo(stack, depth):
    ahead = passed_along(stack[:, :depth], "tx", -1)
    behind = passed_along(stack[:, -depth:], "tx", 1)
    stack = jnp.concatenate([stack, ahead, behind], 1)
    ahead = passed_along(jnp.swapaxes(stack[:, :, :depth], 1, 2), "ty", -1)
    behind = passed_along(jnp.swapaxes(stack[:, :, -depth:], 1, 2), "ty", 1)
    return jnp.concatenate([stack, jnp.swapaxes(ahead, 1, 2), jnp.swapaxes(behind, 1, 2)], 2)


def per_device(orders, offsets, material, e_field, h_field):
    layers, cells_x, cells_y = material.shape
    plane = injection_plane(orders, offsets, cells_x, cells_y)
    coefficient = cell_coefficient(material)
    stack = jnp.concatenate(
        [
            e_field.reshape(3 * layers, cells_x, cells_y),
            h_field.reshape(3 * layers, cells_x, cells_y),
            coefficient,
            plane,
        ],
        0,
    )
    ext = with_halo(stack, STEPS)
    n = 3 * layers
    e_x, e_y, e_z = (ext[i * layers:(i + 1) * layers] for i in range(3))
    h_x, h_y, h_z = (ext[n + i * layers:n + (i + 1) * layers] for i in range(3))
    coefficient = ext[2 * n:2 * n + layers]
    plane_re = ext[2 * n + layers]
    plane_im = ext[2 * n + layers + 1]
    for step in range(STEPS):
        h_x = h_x - COURANT * (fwd(e_z, 2) - fwd(e_y, 0))
        h_y = h_y - COURANT * (fwd(e_x, 0) - fwd(e_z, 1))
        h_z = h_z - COURANT * (fwd(e_y, 1) - fwd(e_x, 2))
        e_x = e_x + coefficient * (bwd(h_z, 2) - bwd(h_y, 0))
        e_y = e_y + coefficient * (bwd(h_x, 0) - bwd(h_z, 1))
        e_z = e_z + coefficient * (bwd(h_y, 1) - bwd(h_x, 2))
        cosine = math.cos(OMEGA * (step + 1))
        sine = math.sin(OMEGA * (step + 1))
        e_x = e_x.at[ZINJ].add(COURANT * (cosine * plane_re - sine * plane_im))
        e_y = e_y.at[ZINJ].add(COURANT * (sine * plane_re + cosine * plane_im))
    crop = lambda f: f[:, :cells_x, :cells_y]
    return (
        jnp.stack([crop(e_x), crop(e_y), crop(e_z)]),
        jnp.stack([crop(h_x), crop(h_y), crop(h_z)]),
    )


def solution(mesh):
    in_specs = (
        P("src", None, "tx", "ty"),
        P("src", None),
        P(None, "tx", "ty"),
        P(None, None, "tx", "ty"),
        P(None, None, "tx", "ty"),
    )
    out_specs = (P(None, None, "tx", "ty"), P(None, None, "tx", "ty"))
    return jax.shard_map(
        per_device, mesh=mesh, in_specs=in_specs, out_specs=out_specs, check_vma=False
    )
```

time: 386 us -> 298 us (0.77); the launches traced: 379 us -> 297 us
  matrix products: 71.6 us -> 6.93 us
  starting transfers between devices: 29.7 us -> 8.49 us
  waiting for transfers between devices: 160 us -> 140 us
  local copies, waits for them, and re-layouts: 60.5 us -> 75.9 us
  other arithmetic: 42.3 us -> 51.6 us
    reduce_scatter x2 -> x0, waiting for transfers between devices: 105 us -> none  [the longest x1 62.9 us: per_device(): lax.psum_scatter(jnp.stack([inner_inner_re, inner_inner_im], 2).reshape(c...]
    all_gather x0 -> x2, waiting for transfers between devices: none -> 99.5 us  [the longest x1 56 us: injection_plane(): inner = lax.all_gather(inner, 'tx', axis=2, tiled=True)]
    dot_general x8, matrix products: 71.6 us -> 6.93 us  [the longest x1 2.37 us: injection_plane(): jnp.einsum('kx,pky->pxy', bx_c, i_im, precision=PREC)]
    ppermute x16 -> x4, starting transfers between devices: 29 us -> 8.37 us  [passed_along(): return lax.ppermute(block, axis, route)]
    another operation x64 -> x1, local copies, waits for them, and re-layouts: 21.7 us -> 1.58 us  [per_device(): jnp.stack([crop(e_x), crop(e_y), crop(e_z)])]
    transpose x0 -> x3, local copies, waits for them, and re-layouts: none -> 17.2 us  [the longest x2 11.7 us: with_halo(): ahead = passed_along(jnp.swapaxes(stack[:, :, :depth], 1, 2), 'ty', -1)]
    ppermute x16 -> x4, waiting for transfers between devices: 19.6 us -> 6.99 us  [passed_along(): return lax.ppermute(block, axis, route)]
    ppermute x0 -> x2, local copies, waits for them, and re-layouts: none -> 9.72 us  [passed_along(): return lax.ppermute(block, axis, route)]
  transfers between devices with their start and end apart: 19 -> 7, of which waited for: 10 -> 5; matrix products, arithmetic and copies ran while one was open for 13% -> 5% of each run, Pallas kernels for 0% -> 0%
where the time goes in v1:
time: 298 us; the launch traced here: 297 us
  waiting for transfers between devices  140 us (47%)
  local copies, waits for them, and re-layouts  75.9 us (25%)
  other arithmetic  51.6 us (17%)
  between operations  14.4 us (5%)
  starting transfers between devices  8.49 us (3%)
  matrix products  6.93 us (2%)
    all_gather x1, waiting for transfers between devices, injection_plane(): inner = lax.all_gather(inner, 'tx', axis=2, tiled=True)  56 us
    all_gather x1, waiting for transfers between devices, injection_plane(): amp = lax.all_gather(orders, 'ty', axis=3, tiled=True)  43.5 us
    psum x1, waiting for transfers between devices, injection_plane(): return lax.psum(plane, 'src')  33.4 us
    slice x27, local copies, waits for them, and re-layouts, fwd(): return jnp.roll(field, -1, axis) - field  15.9 us
    sub x4, other arithmetic, per_device(): h_z = h_z - COURANT * (fwd(e_y, 1) - fwd(e_x, 2))  13.2 us
    transpose x2, local copies, waits for them, and re-layouts, with_halo(): ahead = passed_along(jnp.swapaxes(stack[:, :, :depth], 1, 2), 'ty', -1)  11.7 us
    unnamed x37, local copies, waits for them, and re-layouts  9.9 us
    ppermute x2, local copies, waits for them, and re-layouts, passed_along(): return lax.ppermute(block, axis, route)  9.72 us
  transfers between devices with their start and end apart: 7, of which 5 were waited for; matrix products, arithmetic and copies ran while one was open for 5% of the time, Pallas kernels for 0%

profile of v1, /device:TPU:1, one launch (start us, length us, event | category | flops | bytes accessed | tf_op | source)
XLA Modules:
  0.0 297.1 jit_solution(6683656501134292388)
XLA Ops:
  7.2 1.6 copy.27
  10.9 43.5 %all-gather.3.cloned.1.call-done = f32[4,2,64,512]{2,0,1,3:T(4,128)} async-done(((f32[4,2,64,32]{2,0,1,3:T(4,128)}), f32[4,2,64,512]{2,0,1,3:T(4,128)}) %all-gather.3.cloned.1.call-update) | async-done | bytes 1048592 | tf_op jit(solution)/shard_map/all_gather | solution.py:70
  54.4 1.7 fusion.128
  60.0 56.0 %all-gather.5.cloned.1.call-done = f32[4,2,512,128]{3,2,0,1:T(8,128)} async-done(((f32[4,2,64,128]{3,2,0,1:T(8,128)}), f32[4,2,512,128]{3,2,0,1:T(8,128)}) %all-gather.5.cloned.1.call-update) | async-done | bytes 2097168 | tf_op jit(solution)/shard_map/all_gather | solution.py:85
  116.0 2.4 fusion.75
  118.4 1.0 fusion.74
  119.4 1.0 convolution_subtract_fusion
  120.4 1.0 subtract_reduce_fusion
  122.2 1.5 select_add_fusion
  123.7 33.4 %all-reduce.18.cloned.1.call-done = f32[2,256,128]{1,2,0:T(8,128)} async-done(((f32[2,256,128]{1,2,0:T(8,128)}), f32[2,256,128]{1,2,0:T(8,128)}) %all-reduce.18.cloned.1.call-update) | async-done | bytes 262160 | tf_op jit(solution)/shard_map/psum | solution.py:102
  157.0 1.1 copy.34
  158.1 1.1 pad_maximum_fusion.21
  159.3 4.6 %collective-permute-start = (f32[44,4,128]{2,1,0:T(4,128)S(1)}, f32[44,4,128]{2,1,0:T(4,128)S(1)}, u32[]{:S(2)}, u32[]{:S(2)}) collective-permute-start(f32[44,4,128]{2,1,0:T(4,128)S(1)} %get-tuple-element.134), channel_id=1, source_target_pairs={{16,0},{32,16},{48,32},{64,48},{80,64},{96,80},{112,96},{0,112},{1... | collective-permute-start | bytes 270344 | tf_op jit(solution)/shard_map/ppermute | solution.py:22
  163.9 1.6 collective-permute-done
  165.5 5.4 %collective-permute-done.1 = f32[44,4,128]{2,1,0:T(4,128)S(1)} collective-permute-done((f32[44,4,128]{2,1,0:T(4,128)S(1)}, f32[44,4,128]{2,1,0:T(4,128)S(1)}, u32[]{:S(2)}, u32[]{:S(2)}) %collective-permute-start.1) | collective-permute-done | bytes 90144 | tf_op jit(solution)/shard_map/ppermute | solution.py:22
  170.9 2.1 pad_maximum_fusion.1
  173.0 6.2 %slice_bitcast_fusion.1 = (f32[44,4,264]{1,2,0:T(8,128)}, f32[44,4,264]{1,2,0:T(8,128)}) fusion(f32[44,264,128]{2,1,0:T(8,128)S(1)} %pad_maximum_fusion.1), kind=kLoop, calls=%fused_computation.2 | loop fusion | bytes 743424 | tf_op jit(solution)/shard_map/transpose | solution.py:109
  179.2 5.5 %copy.35 = f32[44,4,264]{2,1,0:T(4,128)} copy(f32[44,4,264]{1,2,0:T(8,128)} %get-tuple-element.132) | data formatting | bytes 371712 | tf_op jit(solution)/shard_map/transpose | solution.py:109
  184.8 2.6 collective-permute-start.2
  187.3 5.5 %copy.37 = f32[44,4,264]{2,1,0:T(4,128)} copy(f32[44,4,264]{1,2,0:T(8,128)} %get-tuple-element.133) | data formatting | bytes 371712 | tf_op jit(solution)/shard_map/transpose | solution.py:110
  192.8 1.2 collective-permute-start.3
  194.0 4.8 %copy.36 = f32[44,4,264]{1,2,0:T(8,128)} copy(f32[44,4,264]{2,1,0:T(4,128)} %collective-permute-done.2) | data formatting | bytes 371712 | tf_op jit(solution)/shard_map/ppermute | solution.py:22
  198.8 4.9 %copy.38 = f32[44,4,264]{1,2,0:T(8,128)} copy(f32[44,4,264]{2,1,0:T(4,128)} %collective-permute-done.3) | data formatting | bytes 371712 | tf_op jit(solution)/shard_map/ppermute | solution.py:22
  203.7 7.5 %pad_maximum_fusion = f32[44,264,136]{2,1,0:T(8,128)S(1)} fusion(f32[44,264,4]{2,1,0:T(8,128)} %bitcast.125, f32[44,264,4]{2,1,0:T(8,128)} %bitcast.124, f32[44,4,128]{2,1,0:T(4,128)} %copy-done.15, f32[44,4,128]{2,1,0:T(4,128)S(1)} %collective-permute-done, f32[2,256,128]{2,1,0:T(8,128)S(1)} %copy.34, f32[6,256,128]{2,1,0:T(8,128)S(1)} %select_add_fusion, ...), kind=kLoop, calls=%fused_computation | loop fusion | flops 11058432 | bytes 12638208 | tf_op jit(solution)/shard_map/concatenate | solution.py:111
  211.4 0.9 fusion.124
  212.3 2.5 copy-done.3
  215.6 1.2 slice.667
  217.1 2.7 fusion.9
  221.5 2.3 fusion.17
  223.8 1.0 slice.674
  225.1 1.0 slice.661
  226.0 1.2 slice.664
  227.3 1.6 slice.660
  229.0 1.7 slice.673
  230.6 1.3 slice.669
  232.6 4.1 %fusion.20 = (f32[6,264,136]{2,1,0:T(8,128)S(1)}, f32[6,264,136]{2,1,0:T(8,128)S(1)}, f32[6,264,136]{2,1,0:T(8,128)S(1)}) fusion(f32[6,264,136]{2,1,0:T(8,128)S(1)} %get-tuple-element.122, f32[6,264,136]{2,1,0:T(8,128)S(1)} %get-tuple-element.120, f32[6,1,136]{2,1,0:T(1,128)S(1)} %slice.659, f32[6,263,136]{2,1,0:T(8,128)S(1)} %slice.658, ...), kind=kLoop, calls=%fused_computation.42 | loop fusion | flops 4093056 | bytes 12638208 | tf_op jit(solution)/shard_map/sub | solution.py:137
  236.8 1.2 slice.662
  238.0 1.2 slice.671
  239.1 1.2 slice.689
  240.3 1.2 slice.676
  241.5 3.5 %fusion.35 = (f32[6,264,136]{2,1,0:T(8,128)S(1)}, f32[6,264,136]{2,1,0:T(8,128)S(1)}, f32[6,264,136]{2,1,0:T(8,128)S(1)}) fusion(f32[6,264,136]{2,1,0:T(8,128)S(1)} %get-tuple-element.120, f32[6,264,136]{2,1,0:T(8,128)S(1)} %get-tuple-element.147, f32[6,263,136]{2,1,0:T(8,128)S(1)} %bitcast.108, f32[6,1,136]{2,1,0:T(1,128)S(1)} %slice.677, ...), kind=kLoop, calls=%fused_computation.64 | loop fusion | flops 4093056 | bytes 13499904 | tf_op jit(solution)/shard_map/add | solution.py:139
  245.0 1.0 slice.696
  246.2 1.0 slice.683
  247.2 1.2 slice.686
  248.5 1.6 slice.682
  250.2 1.7 slice.695
  251.8 1.3 slice.691
  253.1 4.1 %fusion.38 = (f32[6,264,136]{2,1,0:T(8,128)S(1)}, f32[6,264,136]{2,1,0:T(8,128)S(1)}, f32[6,264,136]{2,1,0:T(8,128)S(1)}) fusion(f32[6,264,136]{2,1,0:T(8,128)S(1)} %get-tuple-element.147, f32[6,264,136]{2,1,0:T(8,128)S(1)} %get-tuple-element.118, f32[6,1,136]{2,1,0:T(1,128)S(1)} %slice.681, f32[6,263,136]{2,1,0:T(8,128)S(1)} %slice.680, ...), kind=kLoop, calls=%fused_computation.68 | loop fusion | flops 4093056 | bytes 12638208 | tf_op jit(solution)/shard_map/sub | solution.py:137
  257.3 1.4 slice.684
  258.7 1.2 slice.693
  259.9 1.2 slice.711
  261.1 1.2 slice.698
  263.0 3.5 %fusion.53 = (f32[6,264,136]{2,1,0:T(8,128)S(1)}, f32[6,264,136]{2,1,0:T(8,128)S(1)}, f32[6,264,136]{2,1,0:T(8,128)S(1)}) fusion(f32[6,264,136]{2,1,0:T(8,128)S(1)} %get-tuple-element.118, f32[6,264,136]{2,1,0:T(8,128)S(1)} %get-tuple-element.144, f32[6,263,136]{2,1,0:T(8,128)S(1)} %bitcast.110, f32[6,1,136]{2,1,0:T(1,128)S(1)} %slice.699, ...), kind=kLoop, calls=%fused_computation.90 | loop fusion | flops 4093056 | bytes 13499904 | tf_op jit(solution)/shard_map/add | solution.py:139
  268.3 1.3 copy-done.6
  269.6 2.3 fusion.56
  271.9 1.4 slice.706
  273.4 1.2 slice.728
  274.6 1.2 slice.721
  276.5 5.5 %fusion.59 = (f32[6,264,136]{2,1,0:T(8,128)}, f32[6,264,136]{2,1,0:T(8,128)}, f32[6,264,136]{2,1,0:T(8,128)}) fusion(f32[6,264,136]{2,1,0:T(8,128)S(1)} %get-tuple-element.117, f32[6,264,136]{2,1,0:T(8,128)S(1)} %get-tuple-element.141, f32[6,264,135]{2,1,0:T(8,128)S(1)} %bitcast.117, f32[6,264,1]{2,1,0:T(8,128)} %slice.706, ...), kind=kLoop, calls=%fused_computation.99 | loop fusion | flops 2585088 | bytes 10914816 | tf_op jit(solution)/shard_map/add | solution.py:138
  282.0 2.1 fusion.87
  284.1 1.6 slice_bitcast_fusion.9
  285.7 1.7 slice_bitcast_fusion.11
  287.4 1.6 pad_maximum_fusion.3
  289.0 1.6 pad_maximum_fusion.2
  (99 shorter events, 14.5 us)
Async XLA Ops:
  7.2 47.2 %all-gather.3.cloned.1.call-start = ((), (), s32[]{:S(2)}) async-start(), calls=%async_computation | async-start | bytes 2228224 | tf_op jit(solution)/shard_map/all_gather | solution.py:70
  8.9 107.1 %all-gather.5.cloned.1.call-start = ((), (), s32[]{:S(2)}) async-start(), calls=%async_computation.1 | async-start | bytes 2359296 | tf_op jit(solution)/shard_map/all_gather | solution.py:85
  56.4 1.0 copy-start.14
  59.3 97.8 %all-reduce.18.cloned.1.call-start = ((), (), s32[]{:S(2)}) async-start(), calls=%async_computation.2 | async-start | bytes 524288 | tf_op jit(solution)/shard_map/psum | solution.py:102
  116.0 2.4 copy-start.11
  121.5 36.7 %copy-start.1 = (f32[3,6,256,128]{3,2,1,0:T(8,128)S(1)}, f32[3,6,256,128]{3,2,1,0:T(8,128)}, u32[]{:S(2)}) copy-start(f32[3,6,256,128]{3,2,1,0:T(8,128)} %param.25) | copy-start | bytes 7077892
  158.1 12.8 %copy-start.2 = (f32[3,6,256,128]{3,2,1,0:T(8,128)S(1)}, f32[3,6,256,128]{3,2,1,0:T(8,128)}, u32[]{:S(2)}) copy-start(f32[3,6,256,128]{3,2,1,0:T(8,128)} %param.24) | copy-start | bytes 7077892
  159.3 6.2 %collective-permute-start = (f32[44,4,128]{2,1,0:T(4,128)S(1)}, f32[44,4,128]{2,1,0:T(4,128)S(1)}, u32[]{:S(2)}, u32[]{:S(2)}) collective-permute-start(f32[44,4,128]{2,1,0:T(4,128)S(1)} %get-tuple-element.134), channel_id=1, source_target_pairs={{16,0},{32,16},{48,32},{64,48},{80,64},{96,80},{112,96},{0,112},{1... | collective-permute-start | bytes 270344 | tf_op jit(solution)/shard_map/ppermute | solution.py:22
  163.9 7.0 %collective-permute-start.1 = (f32[44,4,128]{2,1,0:T(4,128)S(1)}, f32[44,4,128]{2,1,0:T(4,128)S(1)}, u32[]{:S(2)}, u32[]{:S(2)}) collective-permute-start(f32[44,4,128]{2,1,0:T(4,128)S(1)} %get-tuple-element.135), channel_id=1, source_target_pairs={{112,0},{0,16},{16,32},{32,48},{48,64},{64,80},{80,96},{96,112},{1... | collective-permute-start | bytes 270344 | tf_op jit(solution)/shard_map/ppermute | solution.py:22
  170.9 2.1 copy-start.15
  184.8 9.2 %collective-permute-start.2 = (f32[44,4,264]{2,1,0:T(4,128)}, f32[44,4,264]{2,1,0:T(4,128)}, u32[]{:S(2)}, u32[]{:S(2)}) collective-permute-start(f32[44,4,264]{2,1,0:T(4,128)} %copy.35), channel_id=1, source_target_pairs={{1,0},{2,1},{3,2},{4,3},{5,4},{6,5},{7,6},{8,7},{9,8},{10,9},{11,1... | collective-permute-start | bytes 557576 | tf_op jit(solution)/shard_map/ppermute | solution.py:22
  192.8 6.0 %collective-permute-start.3 = (f32[44,4,264]{2,1,0:T(4,128)}, f32[44,4,264]{2,1,0:T(4,128)}, u32[]{:S(2)}, u32[]{:S(2)}) collective-permute-start(f32[44,4,264]{2,1,0:T(4,128)} %copy.37), channel_id=1, source_target_pairs={{15,0},{0,1},{1,2},{2,3},{3,4},{4,5},{5,6},{6,7},{7,8},{8,9},{9,10... | collective-permute-start | bytes 557576 | tf_op jit(solution)/shard_map/ppermute | solution.py:22
  211.2 55.4 %copy-start = (f32[44,264,136]{2,1,0:T(8,128)}, f32[44,264,136]{2,1,0:T(8,128)S(1)}, u32[]{:S(2)}) copy-start(f32[44,264,136]{2,1,0:T(8,128)S(1)} %pad_maximum_fusion) | copy-start | bytes 18957316
  211.4 3.4 %copy-start.3 = (f32[3,6,256,128]{3,2,1,0:T(8,128)S(1)}, f32[3,6,256,128]{3,2,1,0:T(8,128)}, u32[]{:S(2)}) copy-start(f32[3,6,256,128]{3,2,1,0:T(8,128)} %param.24) | copy-start | bytes 7077892
  211.4 3.4 %copy-start.16 = (f32[44,4,128]{2,1,0:T(4,128)S(1)}, f32[44,4,128]{2,1,0:T(4,128)}, u32[]{:S(2)}) copy-start(f32[44,4,128]{2,1,0:T(4,128)} %copy-done.15) | copy-start | bytes 270340
  219.8 1.2 copy-start.7
  220.1 1.4 copy-start.13
  230.6 2.0 copy-start.8
  257.3 2.7 copy-start.4
  261.1 1.9 copy-start.5
  268.1 1.4 copy-start.6
  271.9 1.5 copy-start.9
  274.6 1.9 copy-start.10
  284.1 1.6 copy-start.12
Sparse Core Ops, SparseCore 0:
  10.4 43.9 all-gather.2
  59.4 56.5 all-gather.4
  122.3 34.6 all-reduce.17
